TPU v7x, 32 devices: a whole 2x2x4 slice. The times are simulated.
32 devices in a mesh: rows: 16 (over z, y, x), cols: 2 (over core).
Axes of the slice: x: 2, y: 2, z: 4, core: 2. Of those that a mesh axis runs over, the one named last changes fastest.
Arguments:
- quantized: bfloat16 [3072, 384, 128], P('rows', 'cols'), may hold values from 0 to 127, as said below
- scales: bfloat16 [3072, 384], P('rows', 'cols'), may hold values from 0 to 1, as said below
- mode_one: float32 [3072, 32], P('rows'), may hold values from 0 to 40
- mode_two: bfloat16 [384, 32], P('cols'), may hold values from 0 to 1, as said below
- mode_three: bfloat16 [4096, 32], replicated, may hold values from 0 to 0.29882812
- core_tensor: float32 [32, 32, 32], P('rows'), may hold values from 0.0002 to 0.004
- slab_index: int32 [1], replicated, may hold values from 0 to 31
Outputs:
- new_one: float32 [3072, 32], P('rows')
- new_core: float32 [32, 32, 32], P('rows')
Inputs may be any that keep to these rules, and one draw needn't show every extreme that they name: `quantized`: nonnegative integer values of an int8 quantization. `scales`: positive. `mode_two`: nonnegative.
All inputs are finite; a program needn't handle non-finite values.
Results may differ from a plain program's by a relative error of at most 0.0017.
Values sent between devices are 32-bit elements; how exact they have to be, the bound alone decides.
A program may use at most 64 MiB of HBM per device.

v0:
```python
import jax
import jax.numpy as jnp
from jax import lax
from jax.sharding import PartitionSpec as P

SLAB = 128


def weight_gram(core_whole, gram_two, gram_three):
    highest = lax.Precision.HIGHEST
    left = jnp.einsum("rab,ac->rcb", core_whole, gram_two, precision=highest)
    left = jnp.einsum("rcb,bd->rcd", left, gram_three, precision=highest)
    flat = core_whole.reshape(core_whole.shape[0], -1)
    return jnp.dot(left.reshape(flat.shape), flat.T, precision=highest)


def hals_sweep(current, target, coupling):
    highest = lax.Precision.HIGHEST

    def column(position, values):
        where = jnp.asarray(position).astype(jnp.int32)
        weights = lax.dynamic_slice_in_dim(coupling, where, 1, 1)[:, 0]
        diagonal = lax.dynamic_index_in_dim(weights, where, 0, keepdims=False)
        wanted = lax.dynamic_slice_in_dim(target, where, 1, 1)[:, 0]
        before = lax.dynamic_slice_in_dim(values, where, 1, 1)[:, 0]
        fitted = jnp.dot(values, weights, precision=highest)
        after = jnp.maximum(before + (wanted - fitted) / diagonal, 0.0)
        return lax.dynamic_update_slice_in_dim(values, after[:, None], where, 1)

    return lax.fori_loop(0, coupling.shape[0], column, current)


def local(quantized, scales, mode_one, mode_two, mode_three, core_tensor, slab_index):
    highest = lax.Precision.HIGHEST
    whole_core = lax.all_gather(core_tensor, "rows", axis=0, tiled=True)
    flat_core = whole_core.reshape(whole_core.shape[0], -1)
    offset = slab_index[0] * SLAB
    chosen = lax.dynamic_slice_in_dim(mode_three, offset, SLAB, 0)
    tensor = quantized * scales[:, :, None]
    folded = jnp.einsum("jr,ijk->irk", mode_two, tensor, preferred_element_type=jnp.float32).astype(
        jnp.bfloat16
    )
    partial_value = jnp.einsum("irk,ks->irs", folded, chosen, preferred_element_type=jnp.float32)
    partial_value = partial_value.reshape(partial_value.shape[0], -1)
    gram_local = jnp.dot(mode_two.T, mode_two, preferred_element_type=jnp.float32)
    gram_three = jnp.dot(chosen.T, chosen, preferred_element_type=jnp.float32)
    local_target = jnp.dot(partial_value, flat_core.T, precision=highest)
    target, gram_two = lax.psum((local_target, gram_local), "cols")
    coupling = weight_gram(whole_core, gram_two, gram_three)
    updated = hals_sweep(mode_one, target, coupling)
    squares = jnp.sum(updated * updated, axis=0)
    counted = mode_one.shape[0] * lax.axis_size("rows")
    totals = lax.psum(squares, "rows")
    spread = jnp.sqrt(totals / counted + 1e-06)
    normed = updated / spread
    local_rank = core_tensor.shape[0]
    owned = lax.dynamic_slice_in_dim(spread, lax.axis_index("rows") * local_rank, local_rank, 0)
    return (normed, core_tensor * owned[:, None, None])


def solution(mesh):
    in_specs = (
        P("rows", "cols", None),
        P("rows", "cols"),
        P("rows", None),
        P("cols", None),
        P(),
        P("rows", None, None),
        P(),
    )
    out_specs = (P("rows", None), P("rows", None, None))
    return jax.shard_map(local, mesh=mesh, in_specs=in_specs, out_specs=out_specs, check_vma=False)
```

profile of v0, /device:TPU:0, one launch (start us, length us, event | category | flops | bytes accessed | tf_op | source)
XLA Modules:
  0.0 148.8 jit_solution(15536030878287488232)
XLA Ops:
  1.4 8.6 %fusion.10 = bf16[192,32,128]{2,1,0:T(8,128)(2,1)S(1)} fusion(bf16[192,192,128]{2,1,0:T(8,128)(2,1)} %param.9, bf16[192,192]{1,0:T(8,128)(2,1)} %param.10, bf16[192,32]{0,1:T(8,128)(2,1)} %param.12), kind=kOutput, calls=%fused_computation.12 | convolution fusion | flops 321650688 | bytes 11096064 | tf_op jit(solution)/shard_map/jr,ijk->irk/dot_general | solution.py:40
  10.0 1.1 fusion.8
  11.1 45.3 %all_gather.3 = f32[32,32,32]{2,1,0:T(8,128)S(1)} all-gather(f32[2,32,32]{2,1,0:T(8,128)S(1)} %copy-done.2), channel_id=1, replica_groups=mesh['rows'=16,'cols'=2] {'rows'}, dimensions={0}, use_global_device_ids=true | all-gather | bytes 139264 | tf_op jit(solution)/shard_map/all_gather | solution.py:35
  56.5 1.1 convolution_bitcast_fusion.1
  57.7 3.5 %all-reduce = (f32[192,32]{0,1:T(8,128)S(1)}, f32[32,32]{1,0:T(8,128)S(1)}) all-reduce(f32[192,32]{0,1:T(8,128)S(1)} %convolution_bitcast_fusion.1, f32[32,32]{1,0:T(8,128)S(1)} %fusion.24), channel_id=1, replica_groups=mesh['rows'=16,'cols'=2] {'cols'}, use_global_device_ids=true, to_apply=%region_1.0 | all-reduce | flops 7168 | bytes 57344 | tf_op jit(solution)/shard_map/psum | solution.py:48
  62.0 0.9 fusion.13
  62.9 0.8 convolution_bitcast_fusion.2
  63.7 46.9 %while.16 = (s32[]{:T(128)}, f32[192,32]{0,1:T(8,128)S(1)}, f32[192,32]{0,1:T(8,128)S(1)}, f32[32,32]{0,1:T(8,128)S(1)}, s32[]{:T(128)}, /*index=5*/s32[]{:T(128)}, s32[]{:T(128)}) while((s32[]{:T(128)}, f32[192,32]{0,1:T(8,128)S(1)}, f32[192,32]{0,1:T(8,128)S(1)}, f32[32,32]{0,1:T(8,128)S(1)}, s32[]{:T(128)}, /*index=5*/s32[]{:T(128)}, ...), condition=%wide.region_3.4_spmd, body=%wide.region_2.3_spmd.sunk | while | flops 74499 | bytes 41849 | solution.py:30
  64.5 0.7 fusion.37
  65.9 0.7 fusion.37
  67.4 0.7 fusion.37
  68.9 0.7 fusion.37
  70.3 0.7 fusion.37
  71.8 0.7 fusion.37
  73.3 0.7 fusion.37
  74.7 0.7 fusion.37
  76.2 0.7 fusion.37
  77.7 0.7 fusion.37
  79.1 0.7 fusion.37
  80.6 0.7 fusion.37
  82.1 0.7 fusion.37
  83.5 0.7 fusion.37
  85.0 0.7 fusion.37
  89.4 0.7 fusion.37
  90.9 0.7 fusion.37
  92.4 0.7 fusion.37
  104.1 0.7 fusion.37
  105.6 0.7 fusion.37
  107.0 0.7 fusion.37
  110.8 36.6 %psum.23 = f32[32]{0:T(128)S(1)} all-reduce(f32[32]{0:T(128)S(1)} %multiply_reduce_fusion), channel_id=1, replica_groups=mesh['rows'=16,'cols'=2] {'rows'}, use_global_device_ids=true, to_apply=%region_5.6 | all-reduce | flops 32 | bytes 256 | tf_op jit(solution)/shard_map/psum | solution.py:53
  147.4 0.7 broadcast_divide_fusion
  148.1 0.7 broadcast_multiply_fusion
  (153 shorter events, 33.2 us)
Async XLA Ops:
  0.6 9.4 %copy-start = (bf16[4096,32]{0,1:T(8,128)(2,1)S(1)}, bf16[4096,32]{0,1:T(8,128)(2,1)}, u32[]{:S(2)}) copy-start(bf16[4096,32]{0,1:T(8,128)(2,1)} %param.13) | copy-start | bytes 786436
  0.6 56.9 %copy-start.3 = (bf16[192,32]{0,1:T(8,128)(2,1)S(1)}, bf16[192,32]{0,1:T(8,128)(2,1)}, u32[]{:S(2)}) copy-start(bf16[192,32]{0,1:T(8,128)(2,1)} %param.12) | copy-start | bytes 36868
  0.7 10.5 %copy-start.2 = (f32[2,32,32]{2,1,0:T(8,128)S(1)}, f32[2,32,32]{2,1,0:T(8,128)}, u32[]{:S(2)}) copy-start(f32[2,32,32]{2,1,0:T(8,128)} %param.14) | copy-start | bytes 24580
  1.4 62.4 %copy-start.1 = (f32[192,32]{0,1:T(8,128)S(1)}, f32[192,32]{0,1:T(8,128)}, u32[]{:S(2)}) copy-start(f32[192,32]{0,1:T(8,128)} %param.11) | copy-start | bytes 73732
where the time goes:
time: 149 us
  blocking collectives  85.5 us (57%)
  other arithmetic  22.3 us (15%)
  local copies, waits for them, and re-layouts  20.7 us (14%)
  matrix products  17.8 us (12%)
    all_gather x1, blocking collectives, local(): whole_core = lax.all_gather(core_tensor, 'rows', axis=0, tiled=True)  45.3 us
    psum x1, blocking collectives, local(): totals = lax.psum(squares, 'rows')  36.6 us
    max x32, other arithmetic, column(): after = jnp.maximum(before + (wanted - fitted) / diagonal, 0.0)  20.8 us
    dynamic_slice x32, local copies, waits for them, and re-layouts, column(): diagonal = lax.dynamic_index_in_dim(weights, where, 0, keepdims=False)  18.9 us
    dot_general x1, matrix products, local(): jnp.einsum('jr,ijk->irk', mode_two, tensor, preferred_element_type=jnp.fl...  8.62 us
    dot_general x32, matrix products, column(): fitted = jnp.dot(values, weights, precision=highest)  4.4 us
    psum x1, blocking collectives, local(): target, gram_two = lax.psum((local_target, gram_local), 'cols')  3.54 us

commit v1 on v0

--- a/solution.py
+++ b/solution.py
@@ -4,6 +4,27 @@
 from jax.sharding import PartitionSpec as P
 
 SLAB = 128
+
+
+def collect(array, axis, dim):
+    size, index, width = (lax.axis_size(axis), lax.axis_index(axis), array.shape[dim])
+    forward = [(i, (i + 1) % size) for i in range(size)]
+    left = [(i, (i - 1) % size) for i in range(size)]
+    out = jnp.zeros((*array.shape[:dim], size * width, *array.shape[dim + 1 :]), array.dtype)
+    out = lax.dynamic_update_slice_in_dim(out, array, index * width, axis=dim)
+    from_left = from_right = array
+    half = size // 2
+    for step in range(1, half + 1):
+        from_left = lax.ppermute(from_left, axis, forward)
+        out = lax.dynamic_update_slice_in_dim(
+            out, from_left, (index - step) % size * width, axis=dim
+        )
+        if step < size - half:
+            from_right = lax.ppermute(from_right, axis, left)
+            out = lax.dynamic_update_slice_in_dim(
+                out, from_right, (index + step) % size * width, axis=dim
+            )
+    return out
 
 
 def weight_gram(core_whole, gram_two, gram_three):
@@ -32,7 +53,7 @@
 
 def local(quantized, scales, mode_one, mode_two, mode_three, core_tensor, slab_index):
     highest = lax.Precision.HIGHEST
-    whole_core = lax.all_gather(core_tensor, "rows", axis=0, tiled=True)
+    whole_core = collect(core_tensor, "rows", 0)
     flat_core = whole_core.reshape(whole_core.shape[0], -1)
     offset = slab_index[0] * SLAB
     chosen = lax.dynamic_slice_in_dim(mode_three, offset, SLAB, 0)

time: 149 us -> 164 us (1.10)
  blocking collectives: 85.5 us -> 40.1 us
  starting transfers between devices: 0 us -> 41 us
  waiting for transfers between devices: 0 us -> 18 us
    all_gather x1 -> x0, blocking collectives: 45.3 us -> none  [local(): whole_core = lax.all_gather(core_tensor, 'rows', axis=0, tiled=True)]
    ppermute x0 -> x15, starting transfers between devices: none -> 41 us  [the longest x7 37.9 us: collect(): from_right = lax.ppermute(from_right, axis, left)]
    ppermute x0 -> x15, waiting for transfers between devices: none -> 18 us  [the longest x8 18 us: collect(): from_left = lax.ppermute(from_left, axis, forward)]
  transfers between devices with their start and end apart: 0 -> 15, of which waited for: 0 -> 7; matrix products, arithmetic and copies ran while one was open for 0% -> 7% of each run, Pallas kernels for 0% -> 0%
where the time goes in v1:
time: 164 us
  starting transfers between devices  41 us (25%)
  blocking collectives  40.1 us (24%)
  other arithmetic  22.3 us (14%)
  local copies, waits for them, and re-layouts  21.4 us (13%)
  matrix products  18.1 us (11%)
  waiting for transfers between devices  18 us (11%)
  between operations  1.67 us (1%)
    ppermute x7, starting transfers between devices, collect(): from_right = lax.ppermute(from_right, axis, left)  37.9 us
    psum x1, blocking collectives, local(): totals = lax.psum(squares, 'rows')  36.6 us
    max x32, other arithmetic, column(): after = jnp.maximum(before + (wanted - fitted) / diagonal, 0.0)  20.8 us
    dynamic_slice x32, local copies, waits for them, and re-layouts, column(): diagonal = lax.dynamic_index_in_dim(weights, where, 0, keepdims=False)  18.9 us
    ppermute x8, waiting for transfers between devices, collect(): from_left = lax.ppermute(from_left, axis, forward)  18 us
    dot_general x1, matrix products, local(): jnp.einsum('jr,ijk->irk', mode_two, tensor, preferred_element_type=jnp.fl...  8.47 us
    dot_general x32, matrix products, column(): fitted = jnp.dot(values, weights, precision=highest)  4.4 us
    psum x1, blocking collectives, local(): target, gram_two = lax.psum((local_target, gram_local), 'cols')  3.54 us
  transfers between devices with their start and end apart: 15, of which 7 were waited for; matrix products, arithmetic and copies ran while one was open for 7% of the time, Pallas kernels for 0%

profile of v1, /device:TPU:0, one launch (start us, length us, event | category | flops | bytes accessed | tf_op | source)
XLA Modules:
  0.0 163.7 jit_solution(6970327757383597851)
XLA Ops:
  0.7 3.0 %collective-permute-start = (f32[2,32,32]{2,1,0:T(8,128)}, f32[2,32,32]{2,1,0:T(8,128)S(1)}, u32[]{:S(2)}, u32[]{:S(2)}) collective-permute-start(f32[2,32,32]{2,1,0:T(8,128)} %param.14), channel_id=1, source_target_pairs={{0,2},{2,4},{4,6},{6,8},{8,10},{10,12},{12,14},{14,16},{16,18},{18... | collective-permute-start | bytes 24584 | tf_op jit(solution)/shard_map/ppermute | solution.py:18
  3.6 4.1 %collective-permute-start.1 = (f32[2,32,32]{2,1,0:T(8,128)}, f32[2,32,32]{2,1,0:T(8,128)S(1)}, u32[]{:S(2)}, u32[]{:S(2)}) collective-permute-start(f32[2,32,32]{2,1,0:T(8,128)} %param.14), channel_id=1, source_target_pairs={{0,30},{2,0},{4,2},{6,4},{8,6},{10,8},{12,10},{14,12},{16,14},{18,... | collective-permute-start | bytes 24584 | tf_op jit(solution)/shard_map/ppermute | solution.py:23
  8.4 0.9 fusion.23
  9.3 8.5 %fusion.10 = bf16[192,32,128]{2,1,0:T(8,128)(2,1)S(1)} fusion(bf16[192,192,128]{2,1,0:T(8,128)(2,1)} %param.9, bf16[192,192]{1,0:T(8,128)(2,1)} %param.10, bf16[192,32]{0,1:T(8,128)(2,1)} %param.12), kind=kOutput, calls=%fused_computation.12 | convolution fusion | flops 321650688 | bytes 11096064 | tf_op jit(solution)/shard_map/jr,ijk->irk/dot_general | solution.py:61
  17.9 1.1 fusion.8
  19.3 5.6 %collective-permute-start.3 = (f32[2,32,32]{2,1,0:T(8,128)S(1)}, f32[2,32,32]{2,1,0:T(8,128)S(1)}, u32[]{:S(2)}, u32[]{:S(2)}) collective-permute-start(f32[2,32,32]{2,1,0:T(8,128)S(1)} %collective-permute-done.1), channel_id=1, source_target_pairs={{0,30},{2,0},{4,2},{6,4},{8,6},{10,8},{12,10},{14,12},{16,14},{18,... | collective-permute-start | bytes 24584 | tf_op jit(solution)/shard_map/ppermute | solution.py:23
  25.0 1.8 %collective-permute-done.2 = f32[2,32,32]{2,1,0:T(8,128)S(1)} collective-permute-done((f32[2,32,32]{2,1,0:T(8,128)S(1)}, f32[2,32,32]{2,1,0:T(8,128)S(1)}, u32[]{:S(2)}, u32[]{:S(2)}) %collective-permute-start.2) | collective-permute-done | bytes 8224 | tf_op jit(solution)/shard_map/ppermute | solution.py:18
  26.8 5.6 %collective-permute-start.5 = (f32[2,32,32]{2,1,0:T(8,128)S(1)}, f32[2,32,32]{2,1,0:T(8,128)S(1)}, u32[]{:S(2)}, u32[]{:S(2)}) collective-permute-start(f32[2,32,32]{2,1,0:T(8,128)S(1)} %collective-permute-done.3), channel_id=1, source_target_pairs={{0,30},{2,0},{4,2},{6,4},{8,6},{10,8},{12,10},{14,12},{16,14},{18,... | collective-permute-start | bytes 24584 | tf_op jit(solution)/shard_map/ppermute | solution.py:23
  32.5 1.8 %collective-permute-done.4 = f32[2,32,32]{2,1,0:T(8,128)S(1)} collective-permute-done((f32[2,32,32]{2,1,0:T(8,128)S(1)}, f32[2,32,32]{2,1,0:T(8,128)S(1)}, u32[]{:S(2)}, u32[]{:S(2)}) %collective-permute-start.4) | collective-permute-done | bytes 8224 | tf_op jit(solution)/shard_map/ppermute | solution.py:18
  34.3 5.6 %collective-permute-start.7 = (f32[2,32,32]{2,1,0:T(8,128)S(1)}, f32[2,32,32]{2,1,0:T(8,128)S(1)}, u32[]{:S(2)}, u32[]{:S(2)}) collective-permute-start(f32[2,32,32]{2,1,0:T(8,128)S(1)} %collective-permute-done.5), channel_id=1, source_target_pairs={{0,30},{2,0},{4,2},{6,4},{8,6},{10,8},{12,10},{14,12},{16,14},{18,... | collective-permute-start | bytes 24584 | tf_op jit(solution)/shard_map/ppermute | solution.py:23
  40.0 1.8 %collective-permute-done.6 = f32[2,32,32]{2,1,0:T(8,128)S(1)} collective-permute-done((f32[2,32,32]{2,1,0:T(8,128)S(1)}, f32[2,32,32]{2,1,0:T(8,128)S(1)}, u32[]{:S(2)}, u32[]{:S(2)}) %collective-permute-start.6) | collective-permute-done | bytes 8224 | tf_op jit(solution)/shard_map/ppermute | solution.py:18
  41.8 5.6 %collective-permute-start.9 = (f32[2,32,32]{2,1,0:T(8,128)S(1)}, f32[2,32,32]{2,1,0:T(8,128)S(1)}, u32[]{:S(2)}, u32[]{:S(2)}) collective-permute-start(f32[2,32,32]{2,1,0:T(8,128)S(1)} %collective-permute-done.7), channel_id=1, source_target_pairs={{0,30},{2,0},{4,2},{6,4},{8,6},{10,8},{12,10},{14,12},{16,14},{18,... | collective-permute-start | bytes 24584 | tf_op jit(solution)/shard_map/ppermute | solution.py:23
  47.5 1.8 %collective-permute-done.8 = f32[2,32,32]{2,1,0:T(8,128)S(1)} collective-permute-done((f32[2,32,32]{2,1,0:T(8,128)S(1)}, f32[2,32,32]{2,1,0:T(8,128)S(1)}, u32[]{:S(2)}, u32[]{:S(2)}) %collective-permute-start.8) | collective-permute-done | bytes 8224 | tf_op jit(solution)/shard_map/ppermute | solution.py:18
  49.3 5.6 %collective-permute-start.11 = (f32[2,32,32]{2,1,0:T(8,128)S(1)}, f32[2,32,32]{2,1,0:T(8,128)S(1)}, u32[]{:S(2)}, u32[]{:S(2)}) collective-permute-start(f32[2,32,32]{2,1,0:T(8,128)S(1)} %collective-permute-done.9), channel_id=1, source_target_pairs={{0,30},{2,0},{4,2},{6,4},{8,6},{10,8},{12,10},{14,12},{16,14},{18,... | collective-permute-start | bytes 24584 | tf_op jit(solution)/shard_map/ppermute | solution.py:23
  55.1 1.8 %collective-permute-done.10 = f32[2,32,32]{2,1,0:T(8,128)S(1)} collective-permute-done((f32[2,32,32]{2,1,0:T(8,128)S(1)}, f32[2,32,32]{2,1,0:T(8,128)S(1)}, u32[]{:S(2)}, u32[]{:S(2)}) %collective-permute-start.10) | collective-permute-done | bytes 8224 | tf_op jit(solution)/shard_map/ppermute | solution.py:18
  56.9 5.8 %collective-permute-start.13 = (f32[2,32,32]{2,1,0:T(8,128)S(1)}, f32[2,32,32]{2,1,0:T(8,128)S(1)}, u32[]{:S(2)}, u32[]{:S(2)}) collective-permute-start(f32[2,32,32]{2,1,0:T(8,128)S(1)} %collective-permute-done.11), channel_id=1, source_target_pairs={{0,30},{2,0},{4,2},{6,4},{8,6},{10,8},{12,10},{14,12},{16,14},{18,... | collective-permute-start | bytes 24584 | tf_op jit(solution)/shard_map/ppermute | solution.py:23
  62.7 1.6 collective-permute-done.12
  64.5 7.4 %collective-permute-done.14 = f32[2,32,32]{2,1,0:T(8,128)S(1)} collective-permute-done((f32[2,32,32]{2,1,0:T(8,128)S(1)}, f32[2,32,32]{2,1,0:T(8,128)S(1)}, u32[]{:S(2)}, u32[]{:S(2)}) %collective-permute-start.14) | collective-permute-done | bytes 8224 | tf_op jit(solution)/shard_map/ppermute | solution.py:18
  71.9 0.8 convolution_bitcast_fusion.1
  72.8 3.5 %all-reduce = (f32[192,32]{0,1:T(8,128)S(1)}, f32[32,32]{1,0:T(8,128)S(1)}) all-reduce(f32[192,32]{0,1:T(8,128)S(1)} %convolution_bitcast_fusion.1, f32[32,32]{1,0:T(8,128)S(1)} %fusion.23), channel_id=1, replica_groups=mesh['rows'=16,'cols'=2] {'cols'}, use_global_device_ids=true, to_apply=%region_1.2 | all-reduce | flops 7168 | bytes 57344 | tf_op jit(solution)/shard_map/psum | solution.py:69
  76.3 0.9 convolution_bitcast_fusion
  77.2 0.9 fusion.13
  78.6 46.9 %while.16 = (s32[]{:T(128)}, f32[192,32]{0,1:T(8,128)S(1)}, f32[192,32]{0,1:T(8,128)S(1)}, f32[32,32]{0,1:T(8,128)S(1)}, s32[]{:T(128)}, /*index=5*/s32[]{:T(128)}, s32[]{:T(128)}) while((s32[]{:T(128)}, f32[192,32]{0,1:T(8,128)S(1)}, f32[192,32]{0,1:T(8,128)S(1)}, f32[32,32]{0,1:T(8,128)S(1)}, s32[]{:T(128)}, /*index=5*/s32[]{:T(128)}, ...), condition=%wide.region_3.4_spmd, body=%wide.region_2.3_spmd.sunk | while | flops 74499 | bytes 41857 | solution.py:51
  85.3 0.7 fusion.37
  86.7 0.7 fusion.37
  88.2 0.7 fusion.37
  98.5 0.7 fusion.37
  99.9 0.7 fusion.37
  101.4 0.7 fusion.37
  125.7 36.6 %psum.23 = f32[32]{0:T(128)S(1)} all-reduce(f32[32]{0:T(128)S(1)} %multiply_reduce_fusion), channel_id=1, replica_groups=mesh['rows'=16,'cols'=2] {'rows'}, use_global_device_ids=true, to_apply=%region_5.6 | all-reduce | flops 32 | bytes 256 | tf_op jit(solution)/shard_map/psum | solution.py:74
  162.3 0.7 broadcast_divide_fusion
  163.0 0.7 broadcast_multiply_fusion
  (197 shorter events, 43.6 us)
Async XLA Ops:
  0.6 17.3 %copy-start = (bf16[4096,32]{0,1:T(8,128)(2,1)S(1)}, bf16[4096,32]{0,1:T(8,128)(2,1)}, u32[]{:S(2)}) copy-start(bf16[4096,32]{0,1:T(8,128)(2,1)} %param.13) | copy-start | bytes 786436
  0.6 17.2 %copy-start.2 = (f32[2,32,32]{2,1,0:T(8,128)S(1)}, f32[2,32,32]{2,1,0:T(8,128)}, u32[]{:S(2)}) copy-start(f32[2,32,32]{2,1,0:T(8,128)} %param.14) | copy-start | bytes 24580
  0.7 18.6 %collective-permute-start = (f32[2,32,32]{2,1,0:T(8,128)}, f32[2,32,32]{2,1,0:T(8,128)S(1)}, u32[]{:S(2)}, u32[]{:S(2)}) collective-permute-start(f32[2,32,32]{2,1,0:T(8,128)} %param.14), channel_id=1, source_target_pairs={{0,2},{2,4},{4,6},{6,8},{8,10},{10,12},{12,14},{14,16},{16,18},{18... | collective-permute-start | bytes 24584 | tf_op jit(solution)/shard_map/ppermute | solution.py:18
  3.6 15.6 %collective-permute-start.1 = (f32[2,32,32]{2,1,0:T(8,128)}, f32[2,32,32]{2,1,0:T(8,128)S(1)}, u32[]{:S(2)}, u32[]{:S(2)}) collective-permute-start(f32[2,32,32]{2,1,0:T(8,128)} %param.14), channel_id=1, source_target_pairs={{0,30},{2,0},{4,2},{6,4},{8,6},{10,8},{12,10},{14,12},{16,14},{18,... | collective-permute-start | bytes 24584 | tf_op jit(solution)/shard_map/ppermute | solution.py:23
  9.3 69.4 %copy-start.1 = (f32[192,32]{0,1:T(8,128)S(1)}, f32[192,32]{0,1:T(8,128)}, u32[]{:S(2)}) copy-start(f32[192,32]{0,1:T(8,128)} %param.11) | copy-start | bytes 73732
  19.3 7.5 %collective-permute-start.2 = (f32[2,32,32]{2,1,0:T(8,128)S(1)}, f32[2,32,32]{2,1,0:T(8,128)S(1)}, u32[]{:S(2)}, u32[]{:S(2)}) collective-permute-start(f32[2,32,32]{2,1,0:T(8,128)S(1)} %collective-permute-done), channel_id=1, source_target_pairs={{0,2},{2,4},{4,6},{6,8},{8,10},{10,12},{12,14},{14,16},{16,18},{18... | collective-permute-start | bytes 24584 | tf_op jit(solution)/shard_map/ppermute | solution.py:18
  19.3 7.5 %collective-permute-start.3 = (f32[2,32,32]{2,1,0:T(8,128)S(1)}, f32[2,32,32]{2,1,0:T(8,128)S(1)}, u32[]{:S(2)}, u32[]{:S(2)}) collective-permute-start(f32[2,32,32]{2,1,0:T(8,128)S(1)} %collective-permute-done.1), channel_id=1, source_target_pairs={{0,30},{2,0},{4,2},{6,4},{8,6},{10,8},{12,10},{14,12},{16,14},{18,... | collective-permute-start | bytes 24584 | tf_op jit(solution)/shard_map/ppermute | solution.py:23
  26.8 7.5 %collective-permute-start.4 = (f32[2,32,32]{2,1,0:T(8,128)S(1)}, f32[2,32,32]{2,1,0:T(8,128)S(1)}, u32[]{:S(2)}, u32[]{:S(2)}) collective-permute-start(f32[2,32,32]{2,1,0:T(8,128)S(1)} %collective-permute-done.2), channel_id=1, source_target_pairs={{0,2},{2,4},{4,6},{6,8},{8,10},{10,12},{12,14},{14,16},{16,18},{18... | collective-permute-start | bytes 24584 | tf_op jit(solution)/shard_map/ppermute | solution.py:18
  26.8 7.5 %collective-permute-start.5 = (f32[2,32,32]{2,1,0:T(8,128)S(1)}, f32[2,32,32]{2,1,0:T(8,128)S(1)}, u32[]{:S(2)}, u32[]{:S(2)}) collective-permute-start(f32[2,32,32]{2,1,0:T(8,128)S(1)} %collective-permute-done.3), channel_id=1, source_target_pairs={{0,30},{2,0},{4,2},{6,4},{8,6},{10,8},{12,10},{14,12},{16,14},{18,... | collective-permute-start | bytes 24584 | tf_op jit(solution)/shard_map/ppermute | solution.py:23
  34.3 7.5 %collective-permute-start.6 = (f32[2,32,32]{2,1,0:T(8,128)S(1)}, f32[2,32,32]{2,1,0:T(8,128)S(1)}, u32[]{:S(2)}, u32[]{:S(2)}) collective-permute-start(f32[2,32,32]{2,1,0:T(8,128)S(1)} %collective-permute-done.4), channel_id=1, source_target_pairs={{0,2},{2,4},{4,6},{6,8},{8,10},{10,12},{12,14},{14,16},{16,18},{18... | collective-permute-start | bytes 24584 | tf_op jit(solution)/shard_map/ppermute | solution.py:18
  34.3 7.5 %collective-permute-start.7 = (f32[2,32,32]{2,1,0:T(8,128)S(1)}, f32[2,32,32]{2,1,0:T(8,128)S(1)}, u32[]{:S(2)}, u32[]{:S(2)}) collective-permute-start(f32[2,32,32]{2,1,0:T(8,128)S(1)} %collective-permute-done.5), channel_id=1, source_target_pairs={{0,30},{2,0},{4,2},{6,4},{8,6},{10,8},{12,10},{14,12},{16,14},{18,... | collective-permute-start | bytes 24584 | tf_op jit(solution)/shard_map/ppermute | solution.py:23
  41.8 7.5 %collective-permute-start.8 = (f32[2,32,32]{2,1,0:T(8,128)S(1)}, f32[2,32,32]{2,1,0:T(8,128)S(1)}, u32[]{:S(2)}, u32[]{:S(2)}) collective-permute-start(f32[2,32,32]{2,1,0:T(8,128)S(1)} %collective-permute-done.6), channel_id=1, source_target_pairs={{0,2},{2,4},{4,6},{6,8},{8,10},{10,12},{12,14},{14,16},{16,18},{18... | collective-permute-start | bytes 24584 | tf_op jit(solution)/shard_map/ppermute | solution.py:18
  41.8 7.5 %collective-permute-start.9 = (f32[2,32,32]{2,1,0:T(8,128)S(1)}, f32[2,32,32]{2,1,0:T(8,128)S(1)}, u32[]{:S(2)}, u32[]{:S(2)}) collective-permute-start(f32[2,32,32]{2,1,0:T(8,128)S(1)} %collective-permute-done.7), channel_id=1, source_target_pairs={{0,30},{2,0},{4,2},{6,4},{8,6},{10,8},{12,10},{14,12},{16,14},{18,... | collective-permute-start | bytes 24584 | tf_op jit(solution)/shard_map/ppermute | solution.py:23
  49.3 7.5 %collective-permute-start.10 = (f32[2,32,32]{2,1,0:T(8,128)S(1)}, f32[2,32,32]{2,1,0:T(8,128)S(1)}, u32[]{:S(2)}, u32[]{:S(2)}) collective-permute-start(f32[2,32,32]{2,1,0:T(8,128)S(1)} %collective-permute-done.8), channel_id=1, source_target_pairs={{0,2},{2,4},{4,6},{6,8},{8,10},{10,12},{12,14},{14,16},{16,18},{18... | collective-permute-start | bytes 24584 | tf_op jit(solution)/shard_map/ppermute | solution.py:18
  49.3 7.5 %collective-permute-start.11 = (f32[2,32,32]{2,1,0:T(8,128)S(1)}, f32[2,32,32]{2,1,0:T(8,128)S(1)}, u32[]{:S(2)}, u32[]{:S(2)}) collective-permute-start(f32[2,32,32]{2,1,0:T(8,128)S(1)} %collective-permute-done.9), channel_id=1, source_target_pairs={{0,30},{2,0},{4,2},{6,4},{8,6},{10,8},{12,10},{14,12},{16,14},{18,... | collective-permute-start | bytes 24584 | tf_op jit(solution)/shard_map/ppermute | solution.py:23
  56.8 7.5 %collective-permute-start.12 = (f32[2,32,32]{2,1,0:T(8,128)S(1)}, f32[2,32,32]{2,1,0:T(8,128)S(1)}, u32[]{:S(2)}, u32[]{:S(2)}) collective-permute-start(f32[2,32,32]{2,1,0:T(8,128)S(1)} %collective-permute-done.10), channel_id=1, source_target_pairs={{0,2},{2,4},{4,6},{6,8},{8,10},{10,12},{12,14},{14,16},{16,18},{18... | collective-permute-start | bytes 24584 | tf_op jit(solution)/shard_map/ppermute | solution.py:18
  56.9 7.6 %collective-permute-start.13 = (f32[2,32,32]{2,1,0:T(8,128)S(1)}, f32[2,32,32]{2,1,0:T(8,128)S(1)}, u32[]{:S(2)}, u32[]{:S(2)}) collective-permute-start(f32[2,32,32]{2,1,0:T(8,128)S(1)} %collective-permute-done.11), channel_id=1, source_target_pairs={{0,30},{2,0},{4,2},{6,4},{8,6},{10,8},{12,10},{14,12},{16,14},{18,... | collective-permute-start | bytes 24584 | tf_op jit(solution)/shard_map/ppermute | solution.py:23
  64.4 7.5 %collective-permute-start.14 = (f32[2,32,32]{2,1,0:T(8,128)S(1)}, f32[2,32,32]{2,1,0:T(8,128)S(1)}, u32[]{:S(2)}, u32[]{:S(2)}) collective-permute-start(f32[2,32,32]{2,1,0:T(8,128)S(1)} %collective-permute-done.12), channel_id=1, source_target_pairs={{0,2},{2,4},{4,6},{6,8},{8,10},{10,12},{12,14},{14,16},{16,18},{18... | collective-permute-start | bytes 24584 | tf_op jit(solution)/shard_map/ppermute | solution.py:18
